TPU v7x, 32 devices: a whole 2x2x4 slice. The times are simulated.
32 devices in a mesh: gx: 16 (over z, y, x), gy: 2 (over core).
Axes of the slice: x: 2, y: 2, z: 4, core: 2. Of those that a mesh axis runs over, the one named last changes fastest.
Arguments:
- moisture_ratio: float32 [2, 128, 256], P(None, 'gx', 'gy'), may hold values from 11 to 14
- kelvin_warmth: float32 [2, 128, 256], P(None, 'gx', 'gy'), may hold values from 286 to 292
- droplet_size_micron: float32 [8, 2, 128, 256], P(None, None, 'gx', 'gy'), may hold values from 0.5 to 25
- weighting_factor: float32 [8, 2, 128, 256], P(None, None, 'gx', 'gy'), may hold values from 0.1 to 2
- dry_nucleus_size: float32 [8, 2, 128, 256], P(None, None, 'gx', 'gy'), may hold values from 0.02 to 0.3
- fractional_offset_east: float32 [8, 2, 128, 256], P(None, None, 'gx', 'gy'), may hold values from 0 to 1
- fractional_offset_north: float32 [8, 2, 128, 256], P(None, None, 'gx', 'gy'), may hold values from 0 to 1
- encounter_permutation: int32 [8, 2, 128, 256], P(None, None, 'gx', 'gy'), may hold values from 0 to 7, as said below
- departing_eastwest_lists: int32 [16, 2, 2048], P('gx', None, 'gy'), may hold values from -1 to 16383, as said below
- departing_northsouth_lists: int32 [16, 2, 96], P('gx', None, 'gy'), may hold values from -1 to 16383, as said below
- departing_diagonal_lists: int32 [16, 4, 16], P('gx', None, 'gy'), may hold values from -1 to 16383, as said below
Outputs:
- resulting_moisture_ratio: float32 [2, 128, 256], P(None, 'gx', 'gy')
- resulting_kelvin_value: float32 [2, 128, 256], P(None, 'gx', 'gy')
- resulting_droplet_size: float32 [8, 2, 128, 256], P(None, None, 'gx', 'gy')
- resulting_weighting_factor: float32 [8, 2, 128, 256], P(None, None, 'gx', 'gy')
- arrival_particle_records: float32 [5, 16, 4352], P(None, 'gx', 'gy')
- arrival_box_index: int32 [16, 4352], P('gx', 'gy')
Inputs may be any that keep to these rules, and one draw needn't show every extreme that they name: `encounter_permutation`: along the first dimension, the 8 entries of each cell are a permutation of 0 to 7. `departing_eastwest_lists`: each list holds live slot numbers of its own device first and -1 after them, at most 1024 live, and some list of some device is full. Row 0 names only droplets of cells with i = 7, row 1 only i = 0, both only 0 < j < 127. No slot is named twice among all lists of a device. `departing_northsouth_lists`: each list holds live slot numbers of its own device first and -1 after them, at most 48 live, and some list of some device is full. Row 0 names only droplets of cells with j = 127, row 1 only j = 0, both only 0 < i < 7. `departing_diagonal_lists`: each list holds live slot numbers of its own device first and -1 after them, at most 8 live, and some list of some device is full. Row r names only droplets of the corner cell that its move points to: i = 7 for rows 0 and 1, i = 0 for rows 2 and 3, j = 127 for rows 0 and 2, j = 0 for rows 1 and 3.
All inputs are finite; a program needn't handle non-finite values.
Results may differ from a plain program's by a relative error of at most 0.0003.
Values sent between devices are 32-bit elements; how exact they have to be, the bound alone decides.
A program may use at most 64 MiB of HBM per device.

v0:
```python
import jax
import jax.numpy as jnp
from jax import lax
from jax.sharding import PartitionSpec as P

NEWTON = 4


MIX_HORIZONTAL = 0.2
MIX_VERTICAL = 0.05
EXCESS_FACTOR = 4.2222
CURVATURE = 0.0012
KAPPA_SOLUTE = 0.6
GROWTH_STEP = 200.0
COLLIDE_RATE = 4e-07
VAPOUR_PER_SOURCE = 0.001
WARMING_FACTOR = 0.00249


def with_halo(block, sides, width):
    for axis, dim in sides:
        count = lax.axis_size(axis)
        forward = [(i, i + 1) for i in range(count - 1)]
        forward.append((count - 1, 0))
        backward = [(target, source) for source, target in forward]
        low = lax.ppermute(
            lax.slice_in_dim(block, block.shape[dim] - width, None, axis=dim), axis, forward
        )
        high = lax.ppermute(lax.slice_in_dim(block, 0, width, axis=dim), axis, backward)
        block = jnp.concatenate([low, block, high], axis=dim)
    return block


def moisture_excess(moisture_ratio, kelvin_warmth):
    maximum_list_length = EXCESS_FACTOR * jnp.exp(
        17.27 * (kelvin_warmth - 273.15) / (kelvin_warmth - 35.86)
    )
    return moisture_ratio / maximum_list_length - 1.0


def kernel_weights(offset):
    return (
        jnp.maximum(0.5 - offset, 0.0),
        1.0 - jnp.abs(offset - 0.5),
        jnp.maximum(offset - 0.5, 0.0),
    )


def vertical_mix(centre, level_axis):
    levels = centre.shape[level_axis]
    above = jnp.concatenate(
        [
            lax.slice_in_dim(centre, 1, levels, axis=level_axis),
            lax.slice_in_dim(centre, levels - 1, levels, axis=level_axis),
        ],
        level_axis,
    )
    below = jnp.concatenate(
        [
            lax.slice_in_dim(centre, 0, 1, axis=level_axis),
            lax.slice_in_dim(centre, 0, levels - 1, axis=level_axis),
        ],
        level_axis,
    )
    return above + below - 2.0 * centre


def mix_padded(padded):
    centre = padded[:, :, 1:-1, 1:-1]
    horizontal = (
        padded[:, :, 2:, 1:-1]
        + padded[:, :, :-2, 1:-1]
        + padded[:, :, 1:-1, 2:]
        + padded[:, :, 1:-1, :-2]
        - 4.0 * centre
    )
    return centre + MIX_HORIZONTAL * horizontal + MIX_VERTICAL * vertical_mix(centre, 1)


def grow_droplets(droplet_size_micron, dry_nucleus_size, forcing):
    initial = droplet_size_micron * droplet_size_micron
    solute = KAPPA_SOLUTE * dry_nucleus_size * dry_nucleus_size * dry_nucleus_size
    lowest = dry_nucleus_size * dry_nucleus_size
    wetted = initial
    for sweep in range(NEWTON):
        root_wet = jnp.sqrt(wetted)
        inverse = 1.0 / (wetted * root_wet)
        residue = wetted - initial - GROWTH_STEP * (forcing + solute * inverse)
        slope_value = 1.0 + 1.5 * GROWTH_STEP * solute * inverse / wetted
        wetted = jnp.maximum(wetted - residue / slope_value, lowest)
    return wetted


def select_member(values, order_row):
    total = jnp.zeros_like(values[0])
    for member in range(values.shape[0]):
        total = total + jnp.where(order_row == member, values[member], 0.0)
    return total


def coalesce(grown_radius, weighting_factor, encounter_permutation):
    members = encounter_permutation.shape[0]
    new_radius = []
    new_mult = []
    for pair in range(members // 2):
        first_order = encounter_permutation[2 * pair]
        second_order = encounter_permutation[2 * pair + 1]
        first_radius = select_member(grown_radius, first_order)
        second_radius = select_member(grown_radius, second_order)
        first_mult = select_member(weighting_factor, first_order)
        second_mult = select_member(weighting_factor, second_order)
        first_big = first_mult >= second_mult
        high_radius = jnp.where(first_big, first_radius, second_radius)
        low_radius = jnp.where(first_big, second_radius, first_radius)
        high_mult = jnp.where(first_big, first_mult, second_mult)
        low_mult = jnp.where(first_big, second_mult, first_mult)
        radius_sum = first_radius + second_radius
        kernel = (
            COLLIDE_RATE
            * high_mult
            * radius_sum
            * radius_sum
            * jnp.abs(first_radius * first_radius - second_radius * second_radius)
        )
        chance = 1.0 - jnp.exp(-kernel)
        merged_radius = jnp.cbrt(
            low_radius * low_radius * low_radius + chance * high_radius * high_radius * high_radius
        )
        reduced_mult = high_mult - chance * low_mult
        new_radius.append(jnp.where(first_big, high_radius, merged_radius))
        new_radius.append(jnp.where(first_big, merged_radius, high_radius))
        new_mult.append(jnp.where(first_big, reduced_mult, low_mult))
        new_mult.append(jnp.where(first_big, low_mult, reduced_mult))
    out_radius = []
    out_mult = []
    for target in range(members):
        radius_total = jnp.zeros_like(grown_radius[0])
        mult_total = jnp.zeros_like(grown_radius[0])
        for position in range(members):
            hit = encounter_permutation[position] == target
            radius_total = radius_total + jnp.where(hit, new_radius[position], 0.0)
            mult_total = mult_total + jnp.where(hit, new_mult[position], 0.0)
        out_radius.append(radius_total)
        out_mult.append(mult_total)
    return (jnp.stack(out_radius, 0), jnp.stack(out_mult, 0))


def make_records(fields, lists, directions, cells_x, cells_y, levels):
    list_rows = lists.shape[0]
    list_length = lists.shape[1]
    is_live = lists >= 0
    safe_slot = jnp.where(is_live, lists, 0)
    flat_index = safe_slot.reshape(-1)
    picked = jnp.stack(
        [jnp.take(single, flat_index).reshape(list_rows, list_length) for single in fields], 1
    )
    picked = jnp.where(is_live[:, None, :], picked, 0.0)
    cell_index = safe_slot % (levels * cells_x * cells_y)
    level_index = cell_index // (cells_x * cells_y)
    index_x = cell_index // cells_y % cells_x
    index_y = cell_index % cells_y
    move_x = jnp.array([entry[0] for entry in directions], jnp.int32).reshape(list_rows, 1)
    move_y = jnp.array([entry[1] for entry in directions], jnp.int32).reshape(list_rows, 1)
    target = (level_index * cells_x + (index_x + move_x) % cells_x) * cells_y + (
        index_y + move_y
    ) % cells_y
    target = jnp.where(is_live, target, -1).astype(jnp.float32)
    return jnp.concatenate([picked, target[:, None, :]], 1)


def per_device(
    moisture_ratio,
    kelvin_warmth,
    droplet_size_micron,
    weighting_factor,
    dry_nucleus_size,
    fractional_offset_east,
    fractional_offset_north,
    encounter_permutation,
    departing_eastwest_lists,
    departing_northsouth_lists,
    departing_diagonal_lists,
):
    levels = moisture_ratio.shape[0]
    cells_x = moisture_ratio.shape[1]
    cells_y = moisture_ratio.shape[2]
    atmosphere_state_arrays = jnp.stack([moisture_ratio, kelvin_warmth])
    wide_fields = with_halo(atmosphere_state_arrays, (("gx", 2), ("gy", 3)), 2)
    mixed_wide = mix_padded(wide_fields)
    humid_ext = moisture_excess(mixed_wide[0], mixed_wide[1])
    stirred_state_arrays = mixed_wide[:, :, 1:-1, 1:-1]
    weight_x = kernel_weights(fractional_offset_east)
    weight_y = kernel_weights(fractional_offset_north)
    forcing = jnp.zeros_like(droplet_size_micron)
    for shift_x in range(3):
        for shift_y in range(3):
            window = humid_ext[:, shift_x : shift_x + cells_x, shift_y : shift_y + cells_y]
            forcing = forcing + weight_x[shift_x] * weight_y[shift_y] * window[None]
    forcing = forcing - CURVATURE / droplet_size_micron
    wetted = grow_droplets(droplet_size_micron, dry_nucleus_size, forcing)
    condensed = weighting_factor * (
        wetted * jnp.sqrt(wetted) - droplet_size_micron * droplet_size_micron * droplet_size_micron
    )
    source_ext = jnp.zeros((levels, cells_x + 2, cells_y + 2), jnp.float32)
    for shift_x in range(3):
        for shift_y in range(3):
            deposit = jnp.sum(weight_x[shift_x] * weight_y[shift_y] * condensed, axis=0)
            source_ext = source_ext.at[
                :, shift_x : shift_x + cells_x, shift_y : shift_y + cells_y
            ].add(deposit)
    rim_values = with_halo(source_ext, (("gx", 1), ("gy", 2)), 1)
    accumulated_deposition = source_ext[:, 1:-1, 1:-1]
    accumulated_deposition = accumulated_deposition.at[:, 0, :].add(
        rim_values[:, 0, 2 : cells_y + 2]
    )
    accumulated_deposition = accumulated_deposition.at[:, cells_x - 1, :].add(
        rim_values[:, cells_x + 3, 2 : cells_y + 2]
    )
    accumulated_deposition = accumulated_deposition.at[:, :, 0].add(
        rim_values[:, 2 : cells_x + 2, 0]
    )
    accumulated_deposition = accumulated_deposition.at[:, :, cells_y - 1].add(
        rim_values[:, 2 : cells_x + 2, cells_y + 3]
    )
    accumulated_deposition = accumulated_deposition.at[:, 0, 0].add(rim_values[:, 0, 0])
    accumulated_deposition = accumulated_deposition.at[:, cells_x - 1, 0].add(
        rim_values[:, cells_x + 3, 0]
    )
    accumulated_deposition = accumulated_deposition.at[:, 0, cells_y - 1].add(
        rim_values[:, 0, cells_y + 3]
    )
    accumulated_deposition = accumulated_deposition.at[:, cells_x - 1, cells_y - 1].add(
        rim_values[:, cells_x + 3, cells_y + 3]
    )
    resulting_moisture_ratio = stirred_state_arrays[0] - VAPOUR_PER_SOURCE * accumulated_deposition
    resulting_kelvin_value = stirred_state_arrays[1] + WARMING_FACTOR * accumulated_deposition
    grown_radius = jnp.sqrt(wetted)
    resulting_droplet_size, coalesced = coalesce(
        grown_radius, weighting_factor, encounter_permutation
    )
    lists_x = departing_eastwest_lists[0]
    lists_y = departing_northsouth_lists[0]
    lists_corner = departing_diagonal_lists[0]
    slot_count = droplet_size_micron.size
    all_lists = jnp.concatenate(
        [lists_x.reshape(-1), lists_y.reshape(-1), lists_corner.reshape(-1)]
    )
    departed = (
        jnp.zeros((slot_count,), jnp.float32)
        .at[jnp.where(all_lists >= 0, all_lists, slot_count)]
        .set(1.0, mode="drop")
    )
    resulting_weighting_factor = jnp.where(
        departed.reshape(droplet_size_micron.shape) > 0.0, 0.0, coalesced
    )
    fields = (
        resulting_droplet_size.reshape(-1),
        coalesced.reshape(-1),
        dry_nucleus_size.reshape(-1),
        fractional_offset_east.reshape(-1),
        fractional_offset_north.reshape(-1),
    )
    records_x = make_records(fields, lists_x, ((1, 0), (-1, 0)), cells_x, cells_y, levels)
    records_y = make_records(fields, lists_y, ((0, 1), (0, -1)), cells_x, cells_y, levels)
    records_corner = make_records(
        fields, lists_corner, ((1, 1), (1, -1), (-1, 1), (-1, -1)), cells_x, cells_y, levels
    )
    length_x = lists_x.shape[1]
    length_y = lists_y.shape[1]
    length_corner = lists_corner.shape[1]
    east_row = jnp.concatenate([records_x[0], records_corner[0], records_corner[1]], 1)
    west_row = jnp.concatenate([records_x[1], records_corner[2], records_corner[3]], 1)
    got_x = with_halo(jnp.stack([west_row, east_row], 1), (("gx", 1),), 1)
    from_west = got_x[:, 0]
    from_east = got_x[:, 3]
    north_row = jnp.concatenate(
        [
            records_y[0],
            from_west[:, length_x : length_x + length_corner],
            from_east[:, length_x : length_x + length_corner],
        ],
        1,
    )
    south_row = jnp.concatenate(
        [
            records_y[1],
            from_west[:, length_x + length_corner :],
            from_east[:, length_x + length_corner :],
        ],
        1,
    )
    got_y = with_halo(jnp.stack([south_row, north_row], 1), (("gy", 1),), 1)
    from_south = got_y[:, 0]
    from_north = got_y[:, 3]
    south_west = from_south[:, length_y : length_y + length_corner]
    south_east = from_south[:, length_y + length_corner :]
    north_west = from_north[:, length_y : length_y + length_corner]
    north_east = from_north[:, length_y + length_corner :]
    arrivals = jnp.concatenate(
        [
            from_west[:, :length_x],
            from_east[:, :length_x],
            from_south[:, :length_y],
            from_north[:, :length_y],
            south_west,
            south_east,
            north_west,
            north_east,
        ],
        1,
    )
    arrival_particle_records = arrivals[:5][:, None, :]
    arrival_box_index = arrivals[5].astype(jnp.int32)[None, :]
    return (
        resulting_moisture_ratio,
        resulting_kelvin_value,
        resulting_droplet_size,
        resulting_weighting_factor,
        arrival_particle_records,
        arrival_box_index,
    )


def solution(mesh):
    placed = (
        P(None, "gx", "gy"),
        P(None, "gx", "gy"),
        P(None, None, "gx", "gy"),
        P(None, None, "gx", "gy"),
        P(None, None, "gx", "gy"),
        P(None, None, "gx", "gy"),
        P(None, None, "gx", "gy"),
        P(None, None, "gx", "gy"),
        P("gx", None, "gy"),
        P("gx", None, "gy"),
        P("gx", None, "gy"),
    )
    return jax.shard_map(
        per_device,
        mesh=mesh,
        in_specs=placed,
        out_specs=(
            P(None, "gx", "gy"),
            P(None, "gx", "gy"),
            P(None, None, "gx", "gy"),
            P(None, None, "gx", "gy"),
            P(None, "gx", "gy"),
            P("gx", "gy"),
        ),
        check_vma=False,
    )
```

profile of v0, /device:TPU:0, one launch (start us, length us, event | category | flops | bytes accessed | tf_op | source)
XLA Modules:
  0.0 133.6 jit_solution(4000030750198615140)
XLA Ops:
  0.6 0.8 pad_maximum_fusion.13
  1.4 7.0 %collective-permute-start.1 = (f32[2,2,2,128]{3,2,1,0:T(2,128)S(1)}, f32[2,2,2,128]{3,2,1,0:T(2,128)S(1)}, u32[]{:S(2)}, u32[]{:S(2)}) collective-permute-start(f32[2,2,2,128]{3,2,1,0:T(2,128)S(1)} %get-tuple-element.362), channel_id=1, source_target_pairs={{2,0},{4,2},{6,4},{8,6},{10,8},{12,10},{14,12},{16,14},{18,16},{20... | collective-permute-start | bytes 12296 | tf_op jit(solution)/shard_map/ppermute | solution.py:29
  8.4 0.6 copy-done.12
  9.4 0.6 copy-done.11
  10.1 0.2 fusion.84
  10.3 0.6 fusion.137
  10.9 0.6 fusion.136
  11.6 0.7 and_reduce_fusion.1
  12.3 0.7 and_reduce_fusion
  13.0 0.1 concatenate.127
  13.1 11.2 %scatter_custom_fusion = f32[16384]{0:T(1024)S(1)} fusion(s32[2176]{0:T(1024)S(1)} %fusion.49, f32[2176]{0:T(1024)S(1)} %broadcast.4733, f32[]{:T(128)} %constant.715.clone.1), kind=kCustom, calls=%fused_computation.150 | custom fusion | bytes 65540 | tf_op jit(solution)/shard_map/scatter | solution.py:251
  24.4 0.8 copy-done
  25.2 11.8 %gather_fusion.4 = f32[2048]{0:T(1024)S(1)} fusion(f32[16384]{0:T(1024)S(1)} %bitcast.96, s32[2048]{0:T(1024)S(1)} %fusion.93), kind=kCustom, calls=%fused_computation.6.clone | custom fusion | bytes 24576 | tf_op jit(solution)/shard_map/jit(_take)/gather | solution.py:155
  37.0 0.6 copy-done.13
  37.8 0.6 fusion.138
  38.4 11.8 %gather_fusion.2 = f32[2048]{0:T(1024)S(1)} fusion(f32[16384]{0:T(1024)S(1)} %bitcast.105, s32[2048]{0:T(1024)S(1)} %fusion.93), kind=kCustom, calls=%fused_computation.4.clone | custom fusion | bytes 24576 | tf_op jit(solution)/shard_map/jit(_take)/gather | solution.py:155
  50.1 0.7 gather_fusion.9
  50.8 0.7 gather_fusion.7
  51.7 0.5 collective-permute-start.3
  52.2 0.2 copy-done.1
  52.4 11.8 %gather_fusion.3 = f32[2048]{0:T(1024)S(1)} fusion(f32[16384]{0:T(1024)S(1)} %bitcast.99, s32[2048]{0:T(1024)S(1)} %fusion.93), kind=kCustom, calls=%fused_computation.5.clone | custom fusion | bytes 24576 | tf_op jit(solution)/shard_map/jit(_take)/gather | solution.py:155
  64.2 0.7 gather_fusion.8
  64.9 1.1 gather_fusion.14
  66.1 1.1 gather_fusion.12
  67.2 1.1 gather_fusion.13
  68.4 0.1 pad_maximum_fusion.8
  68.6 0.2 fusion.25
  68.9 0.7 copy-done.4
  69.7 0.4 fusion.127
  70.0 0.5 copy-done.5
  70.5 0.1 multiply_reduce_fusion
  70.6 1.4 %fusion.52 = f32[2,8,128]{2,1,0:T(8,128)S(1)} fusion(f32[2,8,128]{2,1,0:T(8,128)S(1)} %get-tuple-element.232, s32[]{:T(128)} %bitcast.4, s32[]{:T(128)} %bitcast.5, f32[2,8,128]{2,1,0:T(8,128)S(1)} %get-tuple-element.233), kind=kLoop, calls=%fused_computation.192 | loop fusion | flops 2048 | bytes 24584 | tf_op jit(solution)/shard_map/add | solution.py:210
  72.0 2.2 %scatter-add.59 = f32[2,10,130]{2,1,0:T(8,128)S(1)} dynamic-update-slice(f32[2,10,130]{2,1,0:T(8,128)S(1)} %scatter-add.56, f32[2,8,128]{2,1,0:T(8,128)S(1)} %fusion.52, s32[]{:T(128)} %constant.752.clone, s32[]{:T(128)} %bitcast.4, s32[]{:T(128)} %bitcast.5) | dynamic-update-slice | bytes 16388 | tf_op jit(solution)/shard_map/scatter-add | solution.py:210
  74.2 2.0 %add_select_fusion = f32[2,8,128]{2,1,0:T(8,128)S(1)} fusion(f32[2,8,128]{2,1,0:T(8,128)S(1)} %get-tuple-element.231, f32[2,10,130]{2,1,0:T(8,128)S(1)} %scatter-add.59, s32[]{:T(128)} %bitcast.6, s32[]{:T(128)} %bitcast.7, pred[]{:T(512)} %and_reduce_fusion.1), kind=kLoop, calls=%fused_computation.183 | loop fusion | flops 4096 | bytes 24585 | tf_op jit(solution)/shard_map/select.19
  76.3 2.2 %scatter-add.60 = f32[2,10,130]{2,1,0:T(8,128)S(1)} dynamic-update-slice(f32[2,10,130]{2,1,0:T(8,128)S(1)} %scatter-add.59, f32[2,8,128]{2,1,0:T(8,128)S(1)} %add_select_fusion, s32[]{:T(128)} %constant.752.clone, s32[]{:T(128)} %bitcast.6, s32[]{:T(128)} %bitcast.7) | dynamic-update-slice | bytes 16388 | tf_op jit(solution)/shard_map/scatter-add | solution.py:210
  78.5 0.5 scatter-add.61
  79.1 0.9 scatter-add.64
  80.1 0.9 scatter-add.65
  81.0 0.5 scatter-add.66
  81.6 0.9 scatter-add.69
  82.6 0.9 scatter-add.70
  83.6 0.2 constant_dynamic-update-slice_fusion.15
  84.0 11.8 %gather_fusion.1 = f32[2048]{0:T(1024)S(1)} fusion(f32[16384]{0:T(1024)S(1)} %bitcast.102, s32[2048]{0:T(1024)S(1)} %fusion.93), kind=kCustom, calls=%fused_computation.3.clone | custom fusion | bytes 24576 | tf_op jit(solution)/shard_map/jit(_take)/gather | solution.py:155
  95.8 0.7 gather_fusion.6
  96.8 11.8 %gather_fusion = f32[2048]{0:T(1024)S(1)} fusion(f32[16384]{0:T(1024)S(1)} %bitcast.108, s32[2048]{0:T(1024)S(1)} %fusion.93), kind=kCustom, calls=%fused_computation.clone | custom fusion | bytes 24576 | tf_op jit(solution)/shard_map/jit(_take)/gather | solution.py:155
  108.6 0.7 gather_fusion.5
  109.3 1.1 gather_fusion.11
  110.4 1.1 gather_fusion.10
  111.7 5.6 %collective-permute-start.5 = (f32[2,1,130]{2,1,0:T(1,128)S(1)}, f32[2,1,130]{2,1,0:T(1,128)S(1)}, u32[]{:S(2)}, u32[]{:S(2)}) collective-permute-start(f32[2,1,130]{2,1,0:T(1,128)S(1)} %get-tuple-element.348), channel_id=1, source_target_pairs={{2,0},{4,2},{6,4},{8,6},{10,8},{12,10},{14,12},{16,14},{18,16},{20... | collective-permute-start | bytes 3128 | tf_op jit(solution)/shard_map/ppermute | solution.py:29
  117.3 0.6 broadcast_select_fusion.1
  118.7 5.6 %collective-permute-start.9 = (f32[6,1,1040]{2,0,1:T(8,128)S(1)}, f32[6,1,1040]{2,0,1:T(8,128)S(1)}, u32[]{:S(2)}, u32[]{:S(2)}) collective-permute-start(f32[6,1,1040]{2,0,1:T(8,128)S(1)} %bitcast.128), channel_id=1, source_target_pairs={{2,0},{4,2},{6,4},{8,6},{10,8},{12,10},{14,12},{16,14},{18,16},{20... | collective-permute-start | bytes 74888 | tf_op jit(solution)/shard_map/ppermute | solution.py:29
  125.0 0.5 collective-permute-start.7
  125.7 0.5 collective-permute-done.6
  126.2 0.1 collective-permute-done.7
  126.4 0.2 scatter-add.76
  126.7 1.9 %broadcast_select_fusion.9 = f32[2,1,1]{2,1,0:T(1,128)S(1)} fusion(pred[]{:T(512)} %and_reduce_fusion, f32[2,12,1]{2,1,0:T(8,128)S(1)} %collective-permute-done.7, f32[2,8,128]{2,1,0:T(8,128)S(1)} %scatter-add.80, s32[]{:T(128)} %bitcast.8, s32[]{:T(128)} %bitcast.9), kind=kLoop, calls=%fused_computation.417 | loop fusion | flops 4 | bytes 33 | tf_op jit(solution)/shard_map/select.32
  128.6 1.4 %scatter-add.81 = f32[2,8,128]{2,1,0:T(8,128)S(1)} dynamic-update-slice(f32[2,8,128]{2,1,0:T(8,128)S(1)} %scatter-add.80, f32[2,1,1]{2,1,0:T(1,128)S(1)} %broadcast_select_fusion.9, s32[]{:T(128)} %constant.752.clone, s32[]{:T(128)} %bitcast.8, s32[]{:T(128)} %bitcast.9) | dynamic-update-slice | bytes 20 | tf_op jit(solution)/shard_map/scatter-add | solution.py:229
  130.1 0.2 scatter-add.84
  130.6 0.3 collective-permute-start.10
  131.0 0.2 collective-permute-start.11
  131.1 0.7 fusion.82
  131.9 0.2 collective-permute-done.11
  132.3 0.6 slice_convert_fusion
  132.9 0.7 copy.26
  (153 shorter events, 4.3 us)
Async XLA Ops:
  1.4 50.1 %collective-permute-start.1 = (f32[2,2,2,128]{3,2,1,0:T(2,128)S(1)}, f32[2,2,2,128]{3,2,1,0:T(2,128)S(1)}, u32[]{:S(2)}, u32[]{:S(2)}) collective-permute-start(f32[2,2,2,128]{3,2,1,0:T(2,128)S(1)} %get-tuple-element.362), channel_id=1, source_target_pairs={{2,0},{4,2},{6,4},{8,6},{10,8},{12,10},{14,12},{16,14},{18,16},{20... | collective-permute-start | bytes 12296 | tf_op jit(solution)/shard_map/ppermute | solution.py:29
  8.4 0.7 copy-start.12
  8.4 0.8 copy-start.10
  8.4 1.0 copy-start.6
  8.4 43.2 %collective-permute-start = (f32[2,2,2,128]{3,2,1,0:T(2,128)S(1)}, f32[2,2,2,128]{3,2,1,0:T(2,128)S(1)}, u32[]{:S(2)}, u32[]{:S(2)}) collective-permute-start(f32[2,2,2,128]{3,2,1,0:T(2,128)S(1)} %get-tuple-element.361), channel_id=1, source_target_pairs={{0,2},{2,4},{4,6},{6,8},{8,10},{10,12},{12,14},{14,16},{16,18},{18... | collective-permute-start | bytes 12296 | tf_op jit(solution)/shard_map/ppermute | solution.py:26
  9.4 0.7 copy-start.11
  10.9 0.7 copy-start.16
  11.6 0.7 copy-start.15
  24.3 0.8 copy-start
  25.2 13.2 %copy-start.2 = (f32[8,2,8,128]{3,2,1,0:T(8,128)S(1)}, f32[8,2,8,128]{3,2,1,0:T(8,128)}, u32[]{:S(2)}) copy-start(f32[8,2,8,128]{3,2,1,0:T(8,128)} %param.61) | copy-start | bytes 196612
  37.0 0.7 copy-start.13
  37.0 0.7 copy-start.14
  50.8 0.7 copy-start.7
  50.8 0.7 copy-start.8
  51.6 0.8 copy-start.1
  51.7 16.7 %collective-permute-start.2 = (f32[2,2,12,2]{3,2,1,0:T(8,128)S(1)}, f32[2,2,12,2]{3,2,1,0:T(8,128)S(1)}, u32[]{:S(2)}, u32[]{:S(2)}) collective-permute-start(f32[2,2,12,2]{3,2,1,0:T(8,128)S(1)} %get-tuple-element.360), channel_id=1, source_target_pairs={{0,1},{1,0},{2,3},{3,2},{4,5},{5,4},{6,7},{7,6},{8,9},{9,8},{10,11... | collective-permute-start | bytes 1160 | tf_op jit(solution)/shard_map/ppermute | solution.py:26
  51.7 16.7 %collective-permute-start.3 = (f32[2,2,12,2]{3,2,1,0:T(8,128)S(1)}, f32[2,2,12,2]{3,2,1,0:T(8,128)S(1)}, u32[]{:S(2)}, u32[]{:S(2)}) collective-permute-start(f32[2,2,12,2]{3,2,1,0:T(8,128)S(1)} %get-tuple-element.359), channel_id=1, source_target_pairs={{1,0},{0,1},{3,2},{2,3},{5,4},{4,5},{7,6},{6,7},{9,8},{8,9},{11,10... | collective-permute-start | bytes 1160 | tf_op jit(solution)/shard_map/ppermute | solution.py:29
  68.8 0.8 copy-start.4
  69.7 0.8 copy-start.5
  81.0 2.6 %copy-start.9 = (s32[8,2,8,128]{3,2,1,0:T(8,128)S(1)}, s32[8,2,8,128]{3,2,1,0:T(8,128)}, u32[]{:S(2)}) copy-start(s32[8,2,8,128]{3,2,1,0:T(8,128)} %param.64) | copy-start | bytes 196612
  96.8 13.7 %copy-start.3 = (f32[8,2,8,128]{3,2,1,0:T(8,128)}, f32[8,2,8,128]{3,2,1,0:T(8,128)S(1)}, u32[]{:S(2)}) copy-start(f32[8,2,8,128]{3,2,1,0:T(8,128)S(1)} %constant_dynamic-update-slice_fusion) | copy-start | bytes 196612
  111.6 13.3 %collective-permute-start.4 = (f32[2,1,130]{2,1,0:T(1,128)S(1)}, f32[2,1,130]{2,1,0:T(1,128)S(1)}, u32[]{:S(2)}, u32[]{:S(2)}) collective-permute-start(f32[2,1,130]{2,1,0:T(1,128)S(1)} %get-tuple-element.349), channel_id=1, source_target_pairs={{0,2},{2,4},{4,6},{6,8},{8,10},{10,12},{12,14},{14,16},{16,18},{18... | collective-permute-start | bytes 3128 | tf_op jit(solution)/shard_map/ppermute | solution.py:26
  111.7 13.2 %collective-permute-start.5 = (f32[2,1,130]{2,1,0:T(1,128)S(1)}, f32[2,1,130]{2,1,0:T(1,128)S(1)}, u32[]{:S(2)}, u32[]{:S(2)}) collective-permute-start(f32[2,1,130]{2,1,0:T(1,128)S(1)} %get-tuple-element.348), channel_id=1, source_target_pairs={{2,0},{4,2},{6,4},{8,6},{10,8},{12,10},{14,12},{16,14},{18,16},{20... | collective-permute-start | bytes 3128 | tf_op jit(solution)/shard_map/ppermute | solution.py:29
  118.6 11.8 %collective-permute-start.8 = (f32[6,1,1040]{2,0,1:T(8,128)S(1)}, f32[6,1,1040]{2,0,1:T(8,128)S(1)}, u32[]{:S(2)}, u32[]{:S(2)}) collective-permute-start(f32[6,1,1040]{2,0,1:T(8,128)S(1)} %bitcast.127), channel_id=1, source_target_pairs={{0,2},{2,4},{4,6},{6,8},{8,10},{10,12},{12,14},{14,16},{16,18},{18... | collective-permute-start | bytes 74888 | tf_op jit(solution)/shard_map/ppermute | solution.py:26
  118.7 11.6 %collective-permute-start.9 = (f32[6,1,1040]{2,0,1:T(8,128)S(1)}, f32[6,1,1040]{2,0,1:T(8,128)S(1)}, u32[]{:S(2)}, u32[]{:S(2)}) collective-permute-start(f32[6,1,1040]{2,0,1:T(8,128)S(1)} %bitcast.128), channel_id=1, source_target_pairs={{2,0},{4,2},{6,4},{8,6},{10,8},{12,10},{14,12},{16,14},{18,16},{20... | collective-permute-start | bytes 74888 | tf_op jit(solution)/shard_map/ppermute | solution.py:29
  125.0 1.2 collective-permute-start.6
  125.0 1.3 %collective-permute-start.7 = (f32[2,12,1]{2,1,0:T(8,128)S(1)}, f32[2,12,1]{2,1,0:T(8,128)S(1)}, u32[]{:S(2)}, u32[]{:S(2)}) collective-permute-start(f32[2,12,1]{2,1,0:T(8,128)S(1)} %get-tuple-element.346), channel_id=1, source_target_pairs={{1,0},{0,1},{3,2},{2,3},{5,4},{4,5},{7,6},{6,7},{9,8},{8,9},{11,10... | collective-permute-start | bytes 296 | tf_op jit(solution)/shard_map/ppermute | solution.py:29
  130.6 1.3 collective-permute-start.10
  131.0 1.2 collective-permute-start.11
where the time goes:
time: 134 us
  local copies, waits for them, and re-layouts  99.5 us (74%)
  starting transfers between devices  19.8 us (15%)
  other arithmetic  12.1 us (9%)
  between operations  1.38 us (1%)
    gather x15, local copies, waits for them, and re-layouts, make_records(): jnp.take(single, flat_index).reshape(list_rows, list_length)  68.1 us
    ppermute x6, starting transfers between devices, with_halo(): lax.ppermute(lax.slice_in_dim(block, 0, width, axis=dim), axis, backward)  19.3 us
    scatter x1, local copies, waits for them, and re-layouts, per_device(): departed = jnp.zeros((slot_count,), jnp.float32).at[jnp.where(all_lists >...  11.2 us
    scatter-add x9, local copies, waits for them, and re-layouts, per_device(): source_ext = source_ext.at[:, shift_x:shift_x + cells_x, shift_y:shift_y...  9.08 us
    another operation x6, other arithmetic  5.29 us
    unnamed x50, local copies, waits for them, and re-layouts  4.98 us
  transfers between devices with their start and end apart: 12, of which 3 were waited for; matrix products, arithmetic and copies ran while one was open for 47% of the time, Pallas kernels for 0%

commit v1 on v0

v1 whole, which is shorter than its diff:
```python
import functools

import jax
import jax.numpy as jnp
from jax import lax
from jax.experimental import pallas as pl
from jax.experimental.pallas import tpu as pltpu
from jax.sharding import PartitionSpec as P

NEWTON = 4
MIX_HORIZONTAL = 0.2
MIX_VERTICAL = 0.05
EXCESS_FACTOR = 4.2222
CURVATURE = 0.0012
KAPPA_SOLUTE = 0.6
GROWTH_STEP = 200.0
COLLIDE_RATE = 4e-07
VAPOUR_PER_SOURCE = 0.001
WARMING_FACTOR = 0.00249

MESH = pl.DeviceIdType.MESH
DIRS = ((1, 0), (-1, 0), (1, 1), (1, -1), (-1, 1), (-1, -1), (0, 1), (0, -1))
SLOT = {d: n for n, d in enumerate(DIRS)}
SHIFTS = (-1, 0, 1)


def div(x, n):
    return lax.shift_right_arithmetic(x, jnp.int32(n.bit_length() - 1))


def mod(x, n):
    return lax.bitwise_and(x, jnp.int32(n - 1))


def iota(shape, dim):
    return lax.broadcasted_iota(jnp.int32, shape, dim)


def kernel_weights(offset):
    return {
        -1: jnp.maximum(0.5 - offset, 0.0),
        0: 1.0 - jnp.abs(offset - 0.5),
        1: jnp.maximum(offset - 0.5, 0.0),
    }


def pieces(x):
    high = x.astype(jnp.bfloat16)
    rest = x - high.astype(jnp.float32)
    middle = rest.astype(jnp.bfloat16)
    low = (rest - middle.astype(jnp.float32)).astype(jnp.bfloat16)
    return high, middle, low


def pick(tables, hot_row, hot_lane):
    rows = tables[0].shape[0]
    split = [pieces(t) for t in tables]
    stacked = jnp.concatenate([s[n] for n in range(3) for s in split], 0)
    got = jnp.dot(stacked, hot_lane, preferred_element_type=jnp.float32)
    third = rows * len(tables)
    got = (got[:third] + got[third : 2 * third]) + got[2 * third :]
    return [
        jnp.sum(jnp.where(hot_row, got[n * rows : (n + 1) * rows], 0.0), 0, keepdims=True)
        for n in range(len(tables))
    ]


def body(
    sizes,
    moist_in, warm_in, size_in, mult_in, dry_in, east_in, north_in, perm_in,
    lx_in, ly_in, lc_in,
    moist_out, warm_out, size_out, mult_out, rec_out, box_out,
    state, drops, perm, lx, ly, lc,
    pack, halo_row, halo_y, dep_out, dep_in,
    rec, recb, edge, edge_in, edge_rec, edge_box,
    mask, new_size, coal, new_mult, final,
    in_sem, out_sem,
    row_send, row_recv, y_send, y_recv, dep_send, dep_recv,
    rec_send, rec_recv, edge_send, edge_recv,
):
    levels, cx, cy, sd, kx, ky, kc, nx, ny = sizes
    me_x = lax.axis_index("gx")
    me_y = lax.axis_index("gy")

    def at(d):
        return (lax.rem(me_x + d[0] + nx, nx), lax.rem(me_y + d[1] + ny, ny))

    barrier = pltpu.get_barrier_semaphore()
    for d in DIRS:
        pl.semaphore_signal(barrier, inc=1, device_id=at(d), device_id_type=MESH)

    loads = []

    def load(source, target):
        copy = pltpu.make_async_copy(source, target, in_sem.at[len(loads)])
        copy.start()
        loads.append(copy)

    load(moist_in, state.at[0])
    load(warm_in, state.at[1])
    load(lx_in.at[0], lx)
    load(ly_in.at[0], ly)
    load(lc_in.at[0], lc)
    for n, source in enumerate((size_in, mult_in, dry_in, east_in, north_in)):
        load(source, drops.at[n])
    load(perm_in, perm)

    loads[0].wait()
    loads[1].wait()
    for f in range(2):
        for l in range(levels):
            q = 2 * (f * levels + l)
            pack[0, q : q + 2, :] = state[f, l, cx - 2 : cx, :]
            pack[1, q : q + 2, :] = state[f, l, 0:2, :]

    pl.semaphore_wait(barrier, len(DIRS))

    sends = []

    def send(source, target, s_sem, r_sem, d):
        copy = pltpu.make_async_remote_copy(
            src_ref=source, dst_ref=target, send_sem=s_sem, recv_sem=r_sem,
            device_id=at(d), device_id_type=MESH,
        )
        copy.start()
        sends.append(copy)
        return copy

    halo = []
    for n in range(6):
        d = DIRS[n]
        halo.append(
            send(pack.at[0 if d[0] > 0 else 1], halo_row.at[n], row_send.at[n], row_recv.at[n], d)
        )
    for n in range(2):
        for f, source in enumerate((moist_in, warm_in)):
            halo.append(
                send(source, halo_y.at[n, f], y_send.at[n, f], y_recv.at[n, f], DIRS[6 + n])
            )

    for copy in loads[2:]:
        copy.wait()
    rows = sd * levels
    block = cx * cy
    hots = []
    mask[...] = jnp.zeros_like(mask)
    for r, (side, dx) in enumerate(((cx - 1, 1), (0, -1))):
        slots = lx[r : r + 1, :]
        j = mod(slots, cy)
        row = div(slots, block)
        hot_row = iota((rows, kx), 0) == row
        hot_lane = jnp.where(iota((cy, kx), 0) == j, 1.0, 0.0).astype(jnp.bfloat16)
        hots.append((hot_row, hot_lane))
        named = lax.dot_general(
            jnp.where(hot_row, 1.0, 0.0).astype(jnp.bfloat16), hot_lane,
            (((1,), (1,)), ((), ())), preferred_element_type=jnp.float32,
        )
        mask[pl.ds(side, rows, stride=cx), :] = named
        static = pick([drops[n, pl.ds(side, rows, stride=cx), :] for n in (2, 3, 4)], hot_row, hot_lane)
        for n in range(3):
            rec[r, 2 + n, :, :] = static[n]
        target = (mod(row, levels) * cx + mod(mod(div(slots, cy), cx) + dx, cx)) * cy + j
        recb[r, :, :] = jnp.where(slots >= 0, target, -1)
        lanes = pl.ds(r * kx, kx)
        send(rec.at[r, 2:5], rec_out.at[2:5, :, lanes], rec_send.at[r, 0], rec_recv.at[r, 0], (dx, 0))
        send(recb.at[r], box_out.at[:, lanes], rec_send.at[r, 1], rec_recv.at[r, 1], (dx, 0))

    width = 2 * ky + 4 * kc
    slots = jnp.concatenate(
        [ly[0:1, :], ly[1:2, :], lc[0:1, :], lc[2:3, :], lc[1:2, :], lc[3:4, :]], 1
    )
    lane_e = iota((1, width), 1)
    high = (lane_e < ky) | ((lane_e >= 2 * ky) & (lane_e < 2 * ky + 2 * kc))
    move_y = jnp.where(high, 1, -1)
    corner = div(lane_e - 2 * ky, kc)
    move_x = jnp.where(lane_e < 2 * ky, 0, jnp.where(mod(corner, 2) == 0, 1, -1))
    target = (
        mod(div(slots, block), levels) * cx + mod(mod(div(slots, cy), cx) + move_x, cx)
    ) * cy + mod(mod(slots, cy) + move_y, cy)
    edge[5:6, :] = jnp.where(slots >= 0, target, -1).astype(jnp.float32)
    named_e = iota((rows * cx, width), 0) == div(slots, cy)
    high_all = jnp.broadcast_to(high, (rows * cx, width))

    def pick_edge(table):
        both = jnp.where(high_all, table[:, cy - 1 : cy], table[:, 0:1])
        return jnp.sum(jnp.where(named_e, both, 0.0), 0, keepdims=True)

    for n in (2, 3, 4):
        edge[n : n + 1, :] = pick_edge(drops[n])
    edge[6:8, :] = jnp.zeros((2, width), jnp.float32)
    hot_e = jnp.where(named_e, 1.0, 0.0)
    left_high = jnp.max(jnp.where(high_all, hot_e, 0.0), 1, keepdims=True)
    left_low = jnp.max(jnp.where(high_all, 0.0, hot_e), 1, keepdims=True)
    lane_all = iota((rows * cx, cy), 1)
    mask[...] = mask[...] + jnp.where(
        lane_all == cy - 1, left_high, jnp.where(lane_all == 0, left_low, 0.0)
    )

    for copy in halo:
        copy.wait_recv()
    wide = []
    for f in range(2):
        wide.append([])
        for l in range(levels):
            q = 2 * (f * levels + l)
            columns = []
            for c in SHIFTS:
                up = pltpu.roll(halo_row[SLOT[(1, -c)]], (cx - 2 - q) % 8, 0)
                down = pltpu.roll(halo_row[SLOT[(-1, -c)]], (8 - q) % 8, 0)
                centre = state[f, l] if c == 0 else halo_y[SLOT[(0, -c)] - 6, f, l]
                columns.append(jnp.concatenate([up, centre, down], 0))
            wide[f].append(jnp.concatenate(columns, 1))
    mixed = []
    for f in range(2):
        mixed.append([])
        for l in range(levels):
            centre = wide[f][l]
            horizontal = (
                pltpu.roll(centre, 3 * cx - 1, 0) + pltpu.roll(centre, 1, 0)
                + pltpu.roll(centre, 3 * cy - 1, 1) + pltpu.roll(centre, 1, 1)
                - 4.0 * centre
            )
            vertical = wide[f][min(l + 1, levels - 1)] + wide[f][max(l - 1, 0)] - 2.0 * centre
            mixed[f].append(centre + MIX_HORIZONTAL * horizontal + MIX_VERTICAL * vertical)
    window = {(a, b): [] for a in SHIFTS for b in SHIFTS}
    for l in range(levels):
        vapour, warmth = mixed[0][l], mixed[1][l]
        humid = vapour / (
            EXCESS_FACTOR * jnp.exp(17.27 * (warmth - 273.15) / (warmth - 35.86))
        ) - 1.0
        for b in SHIFTS:
            column = humid if b == 0 else pltpu.roll(humid, -b % (3 * cy), 1)
            column = column[:, cy : 2 * cy]
            for a in SHIFTS:
                shifted = column if a == 0 else pltpu.roll(column, -a % (3 * cx), 0)
                window[a, b].append(shifted[cx : 2 * cx])
        final[0, l] = vapour[cx : 2 * cx, cy : 2 * cy]
        final[1, l] = warmth[cx : 2 * cx, cy : 2 * cy]
    window = {key: jnp.concatenate(parts, 0) for key, parts in window.items()}

    grown = []
    mult = []
    deposit = {}
    tall = levels * cx
    for k in range(sd):
        part = pl.ds(k * tall, tall)
        radius, weight, dry = drops[0, part, :], drops[1, part, :], drops[2, part, :]
        wx = kernel_weights(drops[3, part, :])
        wy = kernel_weights(drops[4, part, :])
        forcing = -CURVATURE / radius
        for a in SHIFTS:
            across = sum(wy[b] * window[a, b] for b in SHIFTS)
            forcing = forcing + wx[a] * across
        initial = radius * radius
        lowest = dry * dry
        solute = KAPPA_SOLUTE * lowest * dry
        wetted = initial
        for sweep in range(NEWTON):
            inverse_root = lax.rsqrt(wetted)
            inverse_square = inverse_root * inverse_root
            pull = solute * (inverse_square * inverse_root)
            residue = wetted - initial - GROWTH_STEP * (forcing + pull)
            slope = 1.0 + (1.5 * GROWTH_STEP) * pull * inverse_square
            wetted = jnp.maximum(wetted - residue / slope, lowest)
        root = jnp.sqrt(wetted)
        condensed = weight * (wetted * root - initial * radius)
        for a in SHIFTS:
            along = wx[a] * condensed
            for b in SHIFTS:
                term = wy[b] * along
                deposit[a, b] = term if k == 0 else deposit[a, b] + term
        grown.append(root)
        mult.append(weight)

    lane = iota((cx, cy), 1)
    line = iota((cx, cy), 0)

    def spread(parts, size, dim, index):
        back = pltpu.roll(parts[-1], size - 1, dim)
        ahead = pltpu.roll(parts[1], 1, dim)
        inner = parts[0] + jnp.where(index == size - 1, 0.0, back) + jnp.where(index == 0, 0.0, ahead)
        outer = jnp.where(index == size - 1, back, jnp.where(index == 0, ahead, 0.0))
        return inner, outer

    own = []
    for l in range(levels):
        inner, outer = {}, {}
        for a in SHIFTS:
            parts = {b: deposit[a, b][l * cx : (l + 1) * cx] for b in SHIFTS}
            inner[a], outer[a] = spread(parts, cy, 1, lane)
        kept, to_x = spread(inner, cx, 0, line)
        to_y, to_corner = spread(outer, cx, 0, line)
        own.append(kept)
        dep_out[0, l] = to_x
        dep_out[1, l] = to_corner
        dep_out[2, l] = to_y
    deposits = []
    for n, d in enumerate(DIRS):
        kind = 0 if n < 2 else 1 if n < 6 else 2
        deposits.append(send(dep_out.at[kind], dep_in.at[n], dep_send.at[n], dep_recv.at[n], d))

    order = [perm[k * tall : (k + 1) * tall, :] for k in range(sd)]
    hit = [[order[p] == m for m in range(sd)] for p in range(sd)]

    def member(values, p):
        got = values[0]
        for m in range(1, sd):
            got = jnp.where(hit[p][m], values[m], got)
        return got

    after_radius = []
    after_mult = []
    for pair in range(sd // 2):
        p, q = 2 * pair, 2 * pair + 1
        r_p, r_q = member(grown, p), member(grown, q)
        m_p, m_q = member(mult, p), member(mult, q)
        big = m_p >= m_q
        r_hi, r_lo = jnp.where(big, r_p, r_q), jnp.where(big, r_q, r_p)
        m_hi, m_lo = jnp.where(big, m_p, m_q), jnp.where(big, m_q, m_p)
        total = r_p + r_q
        rate = COLLIDE_RATE * m_hi * total * total * jnp.abs(r_p * r_p - r_q * r_q)
        chance = 1.0 - jnp.exp(-rate)
        volume = r_lo * r_lo * r_lo + chance * r_hi * r_hi * r_hi
        merged = jnp.exp(jnp.log(volume) * (1.0 / 3.0))
        reduced = m_hi - chance * m_lo
        after_radius += [jnp.where(big, r_hi, merged), jnp.where(big, merged, r_hi)]
        after_mult += [jnp.where(big, reduced, m_lo), jnp.where(big, m_lo, reduced)]
    for m in range(sd):
        part = pl.ds(m * tall, tall)
        radius, weight = after_radius[0], after_mult[0]
        for p in range(1, sd):
            radius = jnp.where(hit[p][m], after_radius[p], radius)
            weight = jnp.where(hit[p][m], after_mult[p], weight)
        new_size[part, :] = radius
        coal[part, :] = weight
        new_mult[part, :] = jnp.where(mask[part, :] > 0.0, 0.0, weight)

    stores = []

    def store(source, target):
        copy = pltpu.make_async_copy(source, target, out_sem.at[len(stores)])
        copy.start()
        stores.append(copy)

    store(new_size, size_out)
    store(new_mult, mult_out)

    for r, (side, dx) in enumerate(((cx - 1, 1), (0, -1))):
        late = pick([ref[pl.ds(side, rows, stride=cx), :] for ref in (new_size, coal)], *hots[r])
        for n in range(2):
            rec[r, n, :, :] = late[n]
        lanes = pl.ds(r * kx, kx)
        send(rec.at[r, 0:2], rec_out.at[0:2, :, lanes], rec_send.at[r, 2], rec_recv.at[r, 2], (dx, 0))
    edge[0:1, :] = pick_edge(new_size[...])
    edge[1:2, :] = pick_edge(coal[...])
    edges = []
    for n in range(2, 8):
        edges.append(send(edge, edge_in.at[n - 2], edge_send.at[n - 2], edge_recv.at[n - 2], DIRS[n]))

    for copy in deposits:
        copy.wait_recv()
    for l in range(levels):
        total = own[l]
        for n, (dx, dy) in enumerate(DIRS):
            chosen = None
            if dx:
                chosen = line == (0 if dx > 0 else cx - 1)
            if dy:
                there = lane == (0 if dy > 0 else cy - 1)
                chosen = there if chosen is None else chosen & there
            total = total + jnp.where(chosen, dep_in[n, l], 0.0)
        final[0, l] = final[0, l] - VAPOUR_PER_SOURCE * total
        final[1, l] = final[1, l] + WARMING_FACTOR * total
    store(final.at[0], moist_out)
    store(final.at[1], warm_out)

    for copy in edges:
        copy.wait_recv()
    lane_e = iota((8, width), 1)
    came = edge_in[SLOT[(0, 1)] - 2]
    start = ky
    for d, length in (((0, -1), ky), ((1, 1), kc), ((-1, 1), kc), ((1, -1), kc), ((-1, -1), kc)):
        came = jnp.where(lane_e >= start, edge_in[SLOT[d] - 2], came)
        start += length
    for n in range(5):
        edge_rec[n, :, :] = came[n : n + 1, :]
    edge_box[...] = came[5:6, :].astype(jnp.int32)
    store(edge_rec, rec_out.at[:, :, pl.ds(2 * kx, width)])
    store(edge_box, box_out.at[:, pl.ds(2 * kx, width)])

    halo_and_edges = halo + deposits + edges
    for copy in sends:
        if not any(copy is other for other in halo_and_edges):
            copy.wait_recv()
    for copy in sends:
        copy.wait_send()
    for copy in stores:
        copy.wait()


def per_device(nx, ny, moist, warm, size, mult, dry, east, north, perm, lx, ly, lc):
    levels, cx, cy = moist.shape
    sd = size.shape[0]
    kx, ky, kc = lx.shape[2], ly.shape[2], lc.shape[2]
    narr = 2 * kx + 2 * ky + 4 * kc
    width = 2 * ky + 4 * kc
    slots = sd * levels * cx
    flat = [x.reshape(slots, cy) for x in (size, mult, dry, east, north, perm)]
    f32, i32 = jnp.float32, jnp.int32
    any_space = pl.BlockSpec(memory_space=pl.ANY)
    dma = pltpu.SemaphoreType.DMA
    outs = pl.pallas_call(
        functools.partial(body, (levels, cx, cy, sd, kx, ky, kc, nx, ny)),
        out_shape=(
            jax.ShapeDtypeStruct((levels, cx, cy), f32),
            jax.ShapeDtypeStruct((levels, cx, cy), f32),
            jax.ShapeDtypeStruct((slots, cy), f32),
            jax.ShapeDtypeStruct((slots, cy), f32),
            jax.ShapeDtypeStruct((5, 1, narr), f32),
            jax.ShapeDtypeStruct((1, narr), i32),
        ),
        in_specs=[any_space] * 11,
        out_specs=[any_space] * 6,
        scratch_shapes=[
            pltpu.VMEM((2, levels, cx, cy), f32),
            pltpu.VMEM((5, slots, cy), f32),
            pltpu.VMEM((slots, cy), i32),
            pltpu.VMEM((2, kx), i32),
            pltpu.VMEM((2, ky), i32),
            pltpu.VMEM((4, kc), i32),
            pltpu.VMEM((2, 4 * levels, cy), f32),
            pltpu.VMEM((6, 4 * levels, cy), f32),
            pltpu.VMEM((2, 2, levels, cx, cy), f32),
            pltpu.VMEM((3, levels, cx, cy), f32),
            pltpu.VMEM((8, levels, cx, cy), f32),
            pltpu.VMEM((2, 5, 1, kx), f32),
            pltpu.VMEM((2, 1, kx), i32),
            pltpu.VMEM((8, width), f32),
            pltpu.VMEM((6, 8, width), f32),
            pltpu.VMEM((5, 1, width), f32),
            pltpu.VMEM((1, width), i32),
            pltpu.VMEM((slots, cy), f32),
            pltpu.VMEM((slots, cy), f32),
            pltpu.VMEM((slots, cy), f32),
            pltpu.VMEM((slots, cy), f32),
            pltpu.VMEM((2, levels, cx, cy), f32),
            dma((11,)), dma((6,)),
            dma((6,)), dma((6,)), dma((2, 2)), dma((2, 2)), dma((8,)), dma((8,)),
            dma((2, 3)), dma((2, 3)), dma((6,)), dma((6,)),
        ],
        compiler_params=pltpu.CompilerParams(collective_id=0, has_side_effects=True),
    )(moist, warm, *flat, lx, ly, lc)
    return (
        outs[0], outs[1], outs[2].reshape(size.shape), outs[3].reshape(size.shape), outs[4], outs[5],
    )


def solution(mesh):
    cell, drop, lists = P(None, "gx", "gy"), P(None, None, "gx", "gy"), P("gx", None, "gy")
    return jax.shard_map(
        functools.partial(per_device, mesh.shape["gx"], mesh.shape["gy"]),
        mesh=mesh,
        in_specs=(cell,) * 2 + (drop,) * 6 + (lists,) * 3,
        out_specs=(cell, cell, drop, drop, cell, P("gx", "gy")),
        check_vma=False,
    )
```

time: 134 us -> 24.5 us (0.18)
  local copies, waits for them, and re-layouts: 99.5 us -> 5.58 us
  starting transfers between devices: 19.8 us -> 0 us
  Pallas kernels: 0 us -> 17.9 us
  other arithmetic: 12.1 us -> 0 us
    gather x15 -> x0, local copies, waits for them, and re-layouts: 68.1 us -> none  [make_records(): jnp.take(single, flat_index).reshape(list_rows, list_length)]
    ppermute x12 -> x0, starting transfers between devices: 19.8 us -> none  [the longest x6 19.3 us: with_halo(): lax.ppermute(lax.slice_in_dim(block, 0, width, axis=dim), axis, backward)]
    pallas_call x0 -> x1, Pallas kernels: none -> 17.9 us  [per_device(): pl.pallas_call(functools.partial(body, (levels, cx, cy, sd, kx, ky, kc, n...]
    scatter x1 -> x0, local copies, waits for them, and re-layouts: 11.2 us -> none  [per_device(): departed = jnp.zeros((slot_count,), jnp.float32).at[jnp.where(all_lists >...]
    scatter-add x17 -> x0, local copies, waits for them, and re-layouts: 11.1 us -> none  [the longest x9 9.08 us: per_device(): source_ext = source_ext.at[:, shift_x:shift_x + cells_x, shift_y:shift_y...]
    another operation x10 -> x0, other arithmetic: 5.48 us -> none
    add x16 -> x0, other arithmetic: 2.84 us -> none  [the longest x7 1.69 us: per_device(): source_ext = source_ext.at[:, shift_x:shift_x + cells_x, shift_y:shift_y...]
    another operation x17 -> x0, local copies, waits for them, and re-layouts: 2.72 us -> none
  transfers between devices with their start and end apart: 12 -> 0, of which waited for: 3 -> 0; matrix products, arithmetic and copies ran while one was open for 47% -> 0% of each run, Pallas kernels for 0% -> 0%
where the time goes in v1:
time: 24.5 us; the launch traced here: 24.2 us
  Pallas kernels  17.9 us (73%)
  local copies, waits for them, and re-layouts  5.58 us (23%)
  between operations  0.66 us (3%)
    pallas_call x1, Pallas kernels, per_device(): pl.pallas_call(functools.partial(body, (levels, cx, cy, sd, kx, ky, kc, n...  17.9 us
    unnamed x16, local copies, waits for them, and re-layouts  5.58 us

profile of v1, /device:TPU:0, one launch (start us, length us, event | category | flops | bytes accessed | tf_op | source)
XLA Modules:
  0.0 24.2 jit_solution(14303906374424778202)
XLA Ops:
  0.6 17.9 %shard_map.154 = (f32[2,8,128]{2,1,0:T(8,128)}, f32[2,8,128]{2,1,0:T(8,128)}, f32[128,128]{1,0:T(8,128)}, f32[128,128]{1,0:T(8,128)}, f32[5,1,2176]{2,1,0:T(1,128)}, /*index=5*/s32[1,2176]{1,0:T(1,128)}) custom-call(f32[2,8,128]{2,1,0:T(8,128)} %moist_in.1, f32[2,8,128]{2,1,0:T(8,128)} %warm_in.1, f32[128,128]{1,0:T(8,128)} %bitcast.8, f32[128,128]{1,0:T(8,128)} %bitcast.9, ...), custom_call_target="tpu_custom_call" | custom-call | tf_op jit(solution)/shard_map/pallas_call | solution.py:412
  18.6 0.0 copy-start.4
  18.6 0.7 %copy-done.4 = f32[2,8,128]{2,1,0:T(8,128)S(1)} copy-done((f32[2,8,128]{2,1,0:T(8,128)S(1)}, f32[2,8,128]{2,1,0:T(8,128)}, u32[]{:S(2)}) %copy-start.4) | copy-done | bytes 8216
  19.3 0.0 copy-start.3
  19.3 0.6 %copy.23 = f32[2,8,128]{2,1,0:T(8,128)} copy(f32[2,8,128]{2,1,0:T(8,128)S(1)} %copy-done.4) | data formatting | bytes 16384
  19.9 0.1 copy-done.3
  20.0 0.6 %copy.24 = f32[2,8,128]{2,1,0:T(8,128)} copy(f32[2,8,128]{2,1,0:T(8,128)S(1)} %copy-done.3) | data formatting | bytes 16384
  20.6 0.0 copy-start
  20.6 1.5 %copy.25 = f32[8,2,8,128]{3,2,1,0:T(8,128)} copy(f32[8,2,8,128]{3,2,1,0:T(8,128)} %bitcast.15) | data formatting | bytes 131072
  22.1 0.0 copy-done
  22.1 0.0 copy-start.1
  22.1 0.6 %copy.26 = f32[8,2,8,128]{3,2,1,0:T(8,128)} copy(f32[8,2,8,128]{3,2,1,0:T(8,128)S(1)} %bitcast.14) | data formatting | bytes 131072
  22.7 0.2 copy-done.1
  22.9 0.0 copy-start.2
  22.9 0.6 %copy.27 = f32[5,1,2176]{2,1,0:T(1,128)} copy(f32[5,1,2176]{2,1,0:T(1,128)S(1)} %copy-done.1) | data formatting | bytes 87040
  23.5 0.1 copy-done.2
  23.6 0.6 %copy.28 = s32[1,2176]{1,0:T(1,128)} copy(s32[1,2176]{1,0:T(1,128)S(1)} %copy-done.2) | data formatting | bytes 17408
Async XLA Ops:
  18.6 0.7 %copy-start.4 = (f32[2,8,128]{2,1,0:T(8,128)S(1)}, f32[2,8,128]{2,1,0:T(8,128)}, u32[]{:S(2)}) copy-start(f32[2,8,128]{2,1,0:T(8,128)} %get-tuple-element.24) | copy-start | bytes 24580
  19.3 0.7 %copy-start.3 = (f32[2,8,128]{2,1,0:T(8,128)S(1)}, f32[2,8,128]{2,1,0:T(8,128)}, u32[]{:S(2)}) copy-start(f32[2,8,128]{2,1,0:T(8,128)} %get-tuple-element.25) | copy-start | bytes 24580
  20.6 1.5 %copy-start = (f32[128,128]{1,0:T(8,128)S(1)}, f32[128,128]{1,0:T(8,128)}, u32[]{:S(2)}) copy-start(f32[128,128]{1,0:T(8,128)} %get-tuple-element.15) | copy-start | bytes 196612
  22.1 0.8 %copy-start.1 = (f32[5,1,2176]{2,1,0:T(1,128)S(1)}, f32[5,1,2176]{2,1,0:T(1,128)}, u32[]{:S(2)}) copy-start(f32[5,1,2176]{2,1,0:T(1,128)} %get-tuple-element.28) | copy-start | bytes 130564
  22.9 0.7 %copy-start.2 = (s32[1,2176]{1,0:T(1,128)S(1)}, s32[1,2176]{1,0:T(1,128)}, u32[]{:S(2)}) copy-start(s32[1,2176]{1,0:T(1,128)} %get-tuple-element.29) | copy-start | bytes 26116

commit v2 on v1

--- a/solution.py
+++ b/solution.py
@@ -72,9 +72,9 @@
     moist_out, warm_out, size_out, mult_out, rec_out, box_out,
     state, drops, perm, lx, ly, lc,
     pack, halo_row, halo_y, dep_out, dep_in,
-    rec, recb, edge, edge_in, edge_rec, edge_box,
-    mask, new_size, coal, new_mult, final,
-    in_sem, out_sem,
+    rec, recb, edge, edge_in,
+    mask, coal,
+    in_sem,
     row_send, row_recv, y_send, y_recv, dep_send, dep_recv,
     rec_send, rec_recv, edge_send, edge_recv,
 ):
@@ -234,8 +234,8 @@
             for a in SHIFTS:
                 shifted = column if a == 0 else pltpu.roll(column, -a % (3 * cx), 0)
                 window[a, b].append(shifted[cx : 2 * cx])
-        final[0, l] = vapour[cx : 2 * cx, cy : 2 * cy]
-        final[1, l] = warmth[cx : 2 * cx, cy : 2 * cy]
+        moist_out[l] = vapour[cx : 2 * cx, cy : 2 * cy]
+        warm_out[l] = warmth[cx : 2 * cx, cy : 2 * cy]
     window = {key: jnp.concatenate(parts, 0) for key, parts in window.items()}
 
     grown = []
@@ -331,27 +331,17 @@
         for p in range(1, sd):
             radius = jnp.where(hit[p][m], after_radius[p], radius)
             weight = jnp.where(hit[p][m], after_mult[p], weight)
-        new_size[part, :] = radius
+        size_out[part, :] = radius
         coal[part, :] = weight
-        new_mult[part, :] = jnp.where(mask[part, :] > 0.0, 0.0, weight)
-
-    stores = []
-
-    def store(source, target):
-        copy = pltpu.make_async_copy(source, target, out_sem.at[len(stores)])
-        copy.start()
-        stores.append(copy)
-
-    store(new_size, size_out)
-    store(new_mult, mult_out)
+        mult_out[part, :] = jnp.where(mask[part, :] > 0.0, 0.0, weight)
 
     for r, (side, dx) in enumerate(((cx - 1, 1), (0, -1))):
-        late = pick([ref[pl.ds(side, rows, stride=cx), :] for ref in (new_size, coal)], *hots[r])
+        late = pick([ref[pl.ds(side, rows, stride=cx), :] for ref in (size_out, coal)], *hots[r])
         for n in range(2):
             rec[r, n, :, :] = late[n]
         lanes = pl.ds(r * kx, kx)
         send(rec.at[r, 0:2], rec_out.at[0:2, :, lanes], rec_send.at[r, 2], rec_recv.at[r, 2], (dx, 0))
-    edge[0:1, :] = pick_edge(new_size[...])
+    edge[0:1, :] = pick_edge(size_out[...])
     edge[1:2, :] = pick_edge(coal[...])
     edges = []
     for n in range(2, 8):
@@ -369,10 +359,8 @@
                 there = lane == (0 if dy > 0 else cy - 1)
                 chosen = there if chosen is None else chosen & there
             total = total + jnp.where(chosen, dep_in[n, l], 0.0)
-        final[0, l] = final[0, l] - VAPOUR_PER_SOURCE * total
-        final[1, l] = final[1, l] + WARMING_FACTOR * total
-    store(final.at[0], moist_out)
-    store(final.at[1], warm_out)
+        moist_out[l] = moist_out[l] - VAPOUR_PER_SOURCE * total
+        warm_out[l] = warm_out[l] + WARMING_FACTOR * total
 
     for copy in edges:
         copy.wait_recv()
@@ -383,10 +371,8 @@
         came = jnp.where(lane_e >= start, edge_in[SLOT[d] - 2], came)
         start += length
     for n in range(5):
-        edge_rec[n, :, :] = came[n : n + 1, :]
-    edge_box[...] = came[5:6, :].astype(jnp.int32)
-    store(edge_rec, rec_out.at[:, :, pl.ds(2 * kx, width)])
-    store(edge_box, box_out.at[:, pl.ds(2 * kx, width)])
+        rec_out[n, :, pl.ds(2 * kx, width)] = came[n : n + 1, :]
+    box_out[:, pl.ds(2 * kx, width)] = came[5:6, :].astype(jnp.int32)
 
     halo_and_edges = halo + deposits + edges
     for copy in sends:
@@ -394,7 +380,17 @@
             copy.wait_recv()
     for copy in sends:
         copy.wait_send()
-    for copy in stores:
+
+
+def publish(*refs):
+    count = len(refs) // 2
+    sems = refs[-1]
+    copies = [
+        pltpu.make_async_copy(refs[n], refs[count + n], sems.at[n]) for n in range(count)
+    ]
+    for copy in copies:
+        copy.start()
+    for copy in copies:
         copy.wait()
 
 
@@ -408,19 +404,21 @@
     flat = [x.reshape(slots, cy) for x in (size, mult, dry, east, north, perm)]
     f32, i32 = jnp.float32, jnp.int32
     any_space = pl.BlockSpec(memory_space=pl.ANY)
+    vmem_space = pl.BlockSpec(memory_space=pltpu.VMEM)
     dma = pltpu.SemaphoreType.DMA
+    shapes = (
+        ((levels, cx, cy), f32),
+        ((levels, cx, cy), f32),
+        ((slots, cy), f32),
+        ((slots, cy), f32),
+        ((5, 1, narr), f32),
+        ((1, narr), i32),
+    )
     outs = pl.pallas_call(
         functools.partial(body, (levels, cx, cy, sd, kx, ky, kc, nx, ny)),
-        out_shape=(
-            jax.ShapeDtypeStruct((levels, cx, cy), f32),
-            jax.ShapeDtypeStruct((levels, cx, cy), f32),
-            jax.ShapeDtypeStruct((slots, cy), f32),
-            jax.ShapeDtypeStruct((slots, cy), f32),
-            jax.ShapeDtypeStruct((5, 1, narr), f32),
-            jax.ShapeDtypeStruct((1, narr), i32),
-        ),
+        out_shape=tuple(pltpu.VMEM(*s) for s in shapes),
         in_specs=[any_space] * 11,
-        out_specs=[any_space] * 6,
+        out_specs=[vmem_space] * 6,
         scratch_shapes=[
             pltpu.VMEM((2, levels, cx, cy), f32),
             pltpu.VMEM((5, slots, cy), f32),
@@ -437,19 +435,21 @@
             pltpu.VMEM((2, 1, kx), i32),
             pltpu.VMEM((8, width), f32),
             pltpu.VMEM((6, 8, width), f32),
-            pltpu.VMEM((5, 1, width), f32),
-            pltpu.VMEM((1, width), i32),
             pltpu.VMEM((slots, cy), f32),
             pltpu.VMEM((slots, cy), f32),
-            pltpu.VMEM((slots, cy), f32),
-            pltpu.VMEM((slots, cy), f32),
-            pltpu.VMEM((2, levels, cx, cy), f32),
-            dma((11,)), dma((6,)),
+            dma((11,)),
             dma((6,)), dma((6,)), dma((2, 2)), dma((2, 2)), dma((8,)), dma((8,)),
             dma((2, 3)), dma((2, 3)), dma((6,)), dma((6,)),
         ],
         compiler_params=pltpu.CompilerParams(collective_id=0, has_side_effects=True),
     )(moist, warm, *flat, lx, ly, lc)
+    outs = pl.pallas_call(
+        publish,
+        out_shape=tuple(jax.ShapeDtypeStruct(*s) for s in shapes),
+        in_specs=[vmem_space] * 6,
+        out_specs=[any_space] * 6,
+        scratch_shapes=[dma((6,))],
+    )(*[pltpu.with_memory_space_constraint(x, pltpu.VMEM) for x in outs])
     return (
         outs[0], outs[1], outs[2].reshape(size.shape), outs[3].reshape(size.shape), outs[4], outs[5],
     )

time: 24.5 us -> 19 us (0.78)
  local copies, waits for them, and re-layouts: 5.58 us -> 0 us
  Pallas kernels: 17.9 us -> 18.2 us
    unnamed x16 -> x0, local copies, waits for them, and re-layouts: 5.58 us -> none
    pallas_call x0 -> x1, Pallas kernels: none -> 0.73 us  [per_device(): pl.pallas_call(publish, out_shape=tuple((jax.ShapeDtypeStruct(*s) for s i...]
    pallas_call x1, Pallas kernels: 17.9 us -> 17.5 us  [per_device(): pl.pallas_call(functools.partial(body, (levels, cx, cy, sd, kx, ky, kc, n...]
where the time goes in v2:
time: 19 us; the launch traced here: 18.8 us
  Pallas kernels  18.2 us (96%)
  between operations  0.64 us (3%)
    pallas_call x1, Pallas kernels, per_device(): pl.pallas_call(functools.partial(body, (levels, cx, cy, sd, kx, ky, kc, n...  17.5 us
    pallas_call x1, Pallas kernels, per_device(): pl.pallas_call(publish, out_shape=tuple((jax.ShapeDtypeStruct(*s) for s i...  0.73 us

profile of v2, /device:TPU:0, one launch (start us, length us, event | category | flops | bytes accessed | tf_op | source)
XLA Modules:
  0.0 18.8 jit_solution(10436632440046109893)
XLA Ops:
  0.6 17.5 %shard_map.154 = (f32[2,8,128]{2,1,0:T(8,128)S(1)}, f32[2,8,128]{2,1,0:T(8,128)S(1)}, f32[128,128]{1,0:T(8,128)S(1)}, f32[128,128]{1,0:T(8,128)S(1)}, f32[5,1,2176]{2,1,0:T(1,128)S(1)}, /*index=5*/s32[1,2176]{1,0:T(1,128)S(1)}) custom-call(f32[2,8,128]{2,1,0:T(8,128)} %moist_in.1, f32[2,8,128]{2,1,0:T(8,128)} %warm_in.1, f32[128,128]{1,0:T(8,128)} %bitcast.8, ...), custom_call_target="tpu_custom_call" | custom-call | tf_op jit(solution)/shard_map/pallas_call | solution.py:417
  18.1 0.7 %shard_map.155 = (f32[2,8,128]{2,1,0:T(8,128)}, f32[2,8,128]{2,1,0:T(8,128)}, f32[128,128]{1,0:T(8,128)}, f32[128,128]{1,0:T(8,128)}, f32[5,1,2176]{2,1,0:T(1,128)}, /*index=5*/s32[1,2176]{1,0:T(1,128)}) custom-call(f32[2,8,128]{2,1,0:T(8,128)S(1)} %get-tuple-element.18.refs_0_, f32[2,8,128]{2,1,0:T(8,128)S(1)} %get-tuple-element.19.refs_1_, ...), custom_call_target="tpu_custom_call" | custom-call | tf_op jit(solution)/shard_map/pallas_call | solution.py:446

commit v3 on v2

--- a/solution.py
+++ b/solution.py
@@ -71,7 +71,7 @@
     lx_in, ly_in, lc_in,
     moist_out, warm_out, size_out, mult_out, rec_out, box_out,
     state, drops, perm, lx, ly, lc,
-    pack, halo_row, halo_y, dep_out, dep_in,
+    pack, halo_row, halo_y, dep_out, dep_in, dep_rim, rim_in,
     rec, recb, edge, edge_in,
     mask, coal,
     in_sem,
@@ -283,6 +283,7 @@
         return inner, outer
 
     own = []
+    packed = jnp.zeros((cx, cy), jnp.float32)
     for l in range(levels):
         inner, outer = {}, {}
         for a in SHIFTS:
@@ -291,13 +292,13 @@
         kept, to_x = spread(inner, cx, 0, line)
         to_y, to_corner = spread(outer, cx, 0, line)
         own.append(kept)
-        dep_out[0, l] = to_x
-        dep_out[1, l] = to_corner
-        dep_out[2, l] = to_y
+        dep_out[l] = to_y
+        packed = packed + (pltpu.roll(to_x, 2 * l, 0) if l else to_x) + pltpu.roll(to_corner, 2 * (levels + l), 0)
+    dep_rim[...] = packed
     deposits = []
     for n, d in enumerate(DIRS):
-        kind = 0 if n < 2 else 1 if n < 6 else 2
-        deposits.append(send(dep_out.at[kind], dep_in.at[n], dep_send.at[n], dep_recv.at[n], d))
+        source, target = (dep_rim, rim_in.at[n]) if n < 6 else (dep_out, dep_in.at[n - 6])
+        deposits.append(send(source, target, dep_send.at[n], dep_recv.at[n], d))
 
     order = [perm[k * tall : (k + 1) * tall, :] for k in range(sd)]
     hit = [[order[p] == m for m in range(sd)] for p in range(sd)]
@@ -358,7 +359,12 @@
             if dy:
                 there = lane == (0 if dy > 0 else cy - 1)
                 chosen = there if chosen is None else chosen & there
-            total = total + jnp.where(chosen, dep_in[n, l], 0.0)
+            if n < 6:
+                q = l if n < 2 else levels + l
+                came = pltpu.roll(rim_in[n], cx - 2 * q, 0) if q else rim_in[n]
+            else:
+                came = dep_in[n - 6, l]
+            total = total + jnp.where(chosen, came, 0.0)
         moist_out[l] = moist_out[l] - VAPOUR_PER_SOURCE * total
         warm_out[l] = warm_out[l] + WARMING_FACTOR * total
 
@@ -429,8 +435,10 @@
             pltpu.VMEM((2, 4 * levels, cy), f32),
             pltpu.VMEM((6, 4 * levels, cy), f32),
             pltpu.VMEM((2, 2, levels, cx, cy), f32),
-            pltpu.VMEM((3, levels, cx, cy), f32),
-            pltpu.VMEM((8, levels, cx, cy), f32),
+            pltpu.VMEM((levels, cx, cy), f32),
+            pltpu.VMEM((2, levels, cx, cy), f32),
+            pltpu.VMEM((cx, cy), f32),
+            pltpu.VMEM((6, cx, cy), f32),
             pltpu.VMEM((2, 5, 1, kx), f32),
             pltpu.VMEM((2, 1, kx), i32),
             pltpu.VMEM((8, width), f32),

time: 19 us -> 19.1 us (level)
  no operation moved by 1% of the time
where the time goes in v3:
time: 19.1 us; the launch traced here: 18.8 us
  Pallas kernels  18.2 us (95%)
  between operations  0.64 us (3%)
    pallas_call x1, Pallas kernels, per_device(): pl.pallas_call(functools.partial(body, (levels, cx, cy, sd, kx, ky, kc, n...  17.5 us
    pallas_call x1, Pallas kernels, per_device(): pl.pallas_call(publish, out_shape=tuple((jax.ShapeDtypeStruct(*s) for s i...  0.73 us

profile of v3, /device:TPU:0, one launch (start us, length us, event | category | flops | bytes accessed | tf_op | source)
XLA Modules:
  0.0 18.8 jit_solution(2351143906938210540)
XLA Ops:
  0.6 17.5 %shard_map.154 = (f32[2,8,128]{2,1,0:T(8,128)S(1)}, f32[2,8,128]{2,1,0:T(8,128)S(1)}, f32[128,128]{1,0:T(8,128)S(1)}, f32[128,128]{1,0:T(8,128)S(1)}, f32[5,1,2176]{2,1,0:T(1,128)S(1)}, /*index=5*/s32[1,2176]{1,0:T(1,128)S(1)}) custom-call(f32[2,8,128]{2,1,0:T(8,128)} %moist_in.1, f32[2,8,128]{2,1,0:T(8,128)} %warm_in.1, f32[128,128]{1,0:T(8,128)} %bitcast.8, ...), custom_call_target="tpu_custom_call" | custom-call | tf_op jit(solution)/shard_map/pallas_call | solution.py:423
  18.1 0.7 %shard_map.155 = (f32[2,8,128]{2,1,0:T(8,128)}, f32[2,8,128]{2,1,0:T(8,128)}, f32[128,128]{1,0:T(8,128)}, f32[128,128]{1,0:T(8,128)}, f32[5,1,2176]{2,1,0:T(1,128)}, /*index=5*/s32[1,2176]{1,0:T(1,128)}) custom-call(f32[2,8,128]{2,1,0:T(8,128)S(1)} %get-tuple-element.18.refs_0_, f32[2,8,128]{2,1,0:T(8,128)S(1)} %get-tuple-element.19.refs_1_, ...), custom_call_target="tpu_custom_call" | custom-call | tf_op jit(solution)/shard_map/pallas_call | solution.py:454
